TPU v7x, 32 devices: a whole 2x2x4 slice. The times are simulated.
32 devices in a mesh: batch: 4 (over z), head: 4 (over y, x), ctx: 2 (over core).
Axes of the slice: x: 2, y: 2, z: 4, core: 2. Of those that a mesh axis runs over, the one named last changes fastest.
Arguments:
- hidden_in: bfloat16 [4, 1024, 960], P('batch', 'ctx'), may hold values from -6 to 6
- cotangent: bfloat16 [4, 1024, 960], P('batch', 'ctx'), may hold values from -6 to 6
- lengths: int32 [4], P('batch'), may hold values from 64 to 1024, as said below
- owners: int32 [5], replicated, may hold values from 0 to 3, as said below
- w_query: bfloat16 [960, 960], replicated, may hold values from -0.1875 to 0.1875
- w_key: bfloat16 [960, 320], replicated, may hold values from -0.1875 to 0.1875
- w_value: bfloat16 [960, 320], replicated, may hold values from -0.1875 to 0.1875
- w_output: bfloat16 [960, 960], replicated, may hold values from -2 to 2
- gate_weight: bfloat16 [960, 2560], P(None, 'head'), may hold values from -0.1875 to 0.1875
- up_weight: bfloat16 [960, 2560], P(None, 'head'), may hold values from -0.1875 to 0.1875
- down_weight: bfloat16 [2560, 960], P('head'), may hold values from -0.125 to 0.125
- gain_attn: float32 [960], replicated, may hold values from 0.1 to 1.9
- gain_ffn: float32 [960], replicated, may hold values from 0.1 to 1.9
Outputs:
- output: bfloat16 [4, 1024, 960], P('batch', 'ctx')
- grad_input: float32 [4, 1024, 960], P('batch', 'ctx')
- grad_query: float32 [960, 1536], P(None, 'head')
- grad_key: float32 [960, 512], P(None, 'head')
- grad_value: float32 [960, 512], P(None, 'head')
- grad_output: float32 [1536, 960], P('head')
- grad_gate: float32 [960, 2560], P(None, 'head')
- grad_up: float32 [960, 2560], P(None, 'head')
- grad_down: float32 [2560, 960], P('head')
- grad_gain_attn: float32 [960], replicated
- grad_gain_ffn: float32 [960], replicated
Inputs may be any that keep to these rules, and one draw needn't show every extreme that they name: `lengths`: at least one sequence has all 1024 slots valid. `owners`: every head index computes one or two groups.
All inputs are finite; a program needn't handle non-finite values.
Results may differ from a plain program's by a relative error of at most 0.034.
Values may be sent and summed in bfloat16 or wider, within the bound.
A program may use at most 192 MiB of HBM per device.

v0:
```python
import functools
import math
from types import SimpleNamespace

import jax
import jax.numpy as jnp
import numpy as np
from jax import lax
from jax.experimental import pallas as pl
from jax.experimental.pallas import tpu as pltpu
from jax.sharding import PartitionSpec as P

KV = 5
HD = 64
GQ = 3
QH = KV * GQ
HEADS = 4
EPS = 1e-05
NEG = -1e30
MESH = pl.DeviceIdType.MESH
F32 = jnp.float32
BF16 = jnp.bfloat16


def nn(a, b):
    return lax.dot_general(a, b, (((1,), (0,)), ((), ())), preferred_element_type=F32)


def nt(a, b):
    return lax.dot_general(a, b, (((1,), (1,)), ((), ())), preferred_element_type=F32)


def tn(a, b):
    return lax.dot_general(a, b, (((0,), (0,)), ((), ())), preferred_element_type=F32)


def rope_table(slots):
    inverse = np.exp(np.arange(HD // 2, dtype=np.float32) * np.float32(-2.0 * math.log(10000.0) / HD))
    angles = np.arange(slots, dtype=np.float32)[:, None] * inverse[None, :].astype(np.float32)
    cos, sin = np.cos(angles).astype(np.float32), np.sin(angles).astype(np.float32)
    return np.concatenate([cos, sin] * 2, axis=1)


def peer_of(h, j):
    return (h, h + 1 - 2 * (h % 2), (h + 2) % 4, 3 - h)[j]


def scratch_of(rows, d, ff, nb):
    n = HEADS
    half = n * rows
    keys = 2 * half
    dp = -(-d // 128) * 128
    cr = d // 8
    v = pltpu.VMEM
    dma = pltpu.SemaphoreType.DMA
    return dict(
        cot_v=v((d, half), BF16),
        tab_v=v((rows, 256), F32),
        gains_v=v((2, 1, d), F32),
        wq_v=v((d, QH * HD), BF16),
        wk_v=v((KV * HD, d), BF16),
        wv_v=v((KV * HD, d), BF16),
        wo_v=v((QH * HD, d), BF16),
        wf=v((3 * d, ff), BF16),
        res=v((2, rows, d), F32),
        mid=v((2, rows, d), F32),
        nat=v((2, d, rows), BF16),
        dat=v((2, d, rows), BF16),
        ql=v((2, KV, GQ * rows, 128), BF16),
        kv=v((2, KV, keys, 128), BF16),
        lse=v((2, rows, 128), F32),
        at=v((rows, d), BF16),
        nf=v((2, n, rows, d), BF16),
        gate=v((2, n, rows, ff), F32),
        up=v((2, n, rows, ff), F32),
        act=v((n, rows, ff), BF16),
        bias=v((rows, keys), F32),
        wide=v((rows, dp), F32),
        heads=v((QH, rows, 128), F32),
        part=v((2, rows, d), BF16),
        psend=v((2, 3, rows, d), BF16),
        precv=v((2, 3, rows, d), BF16),
        d_res=v((rows, d), F32),
        d_mid=v((rows, d), F32),
        df=v((2, n, rows, d), BF16),
        dg=v((n, rows, ff), BF16),
        du=v((n, rows, ff), BF16),
        ou=v((KV, GQ * rows, 128), BF16),
        dk=v((rows, KV * HD), BF16),
        dv=v((rows, KV * HD), BF16),
        dpg=v((KV, 2 * rows, 384), BF16),
        aog=v((KV, 2 * rows, 256), BF16),
        dkv=v((KV, 128, half), F32),
        dkv_ctx=v((KV, 128, half), BF16),
        dkv_ctx_r=v((2, KV, 128, half), BF16),
        dkv_s=v((KV, 3, 128, rows), BF16),
        dkv_r=v((KV, 3, 128, rows), BF16),
        fin=v((2, d, rows), BF16),
        gown=v((12, cr, ff), F32),
        sf=v((12, cr, ff), BF16),
        rf=v((12, cr, ff), BF16),
        rf2=v((12, cr, ff), BF16),
        zs=v((16, cr, ff), BF16),
        zu=v((16, cr, ff), BF16),
        zb=v((16, cr, ff), BF16),
        ha=v((KV, d // 2, 512), BF16),
        ra=v((KV, d // 2, 512), BF16),
        gain_v=v((2, 1, d), F32),
        gain_p=v((2 * n, 2, 1, d), F32),
        gain_z=v((nb, 2, 1, d), F32),
        in_sem=dma((12,)),
        loc_sem=dma((8,)),
        kv_ss=dma((2, KV)),
        kv_rs=dma((2, KV)),
        kvc_ss=dma((2, KV)),
        kvc_rs=dma((2, KV)),
        ag_ss=dma((5, 6)),
        ag_rs=dma((5, 6)),
        p_ss=dma((4, 4)),
        p_rs=dma((4, 4)),
        dc_ss=dma((2, KV)),
        dc_rs=dma((2, KV)),
        dkv_ss=dma((2, KV)),
        dkv_rs=dma((2, KV)),
        f_ss=dma((3,)),
        f_rs=dma((3,)),
        z_s0=dma((16,)),
        z_s1=dma((16,)),
        z_ur=dma((16,)),
        z_br=dma((16,)),
        og_loc=dma((16,)),
        og_ss=dma((16,)),
        og_rs=dma((16,)),
        a_ss=dma((KV,)),
        a_rs=dma((KV,)),
        h_ss=dma((4, 4)),
        h_rs=dma((4, 4)),
        ex_loc=dma((4,)),
        ex_ss=dma((4, 8)),
        ex_rs=dma((4, 8)),
        gp_ss=dma((8,)),
        gp_rs=dma((8,)),
        gz_ss=dma((nb,)),
        gz_rs=dma((nb,)),
    )


def step_kernel(names, rows, d, ff, nb, *refs):
    r = SimpleNamespace(**dict(zip(names, refs)))
    wg_v, wu_v, wd_v = (r.wf.at[pl.ds(t * d, d)] for t in range(3))
    lhs, hid_v = r.cot_v, r.fin.at[1]
    h = lax.axis_index("head")
    c = lax.axis_index("ctx")
    z = lax.axis_index("batch")
    half = HEADS * rows
    hd2 = d // 2
    cr = d // 8
    lane = lax.broadcasted_iota(jnp.int32, (rows, 128), 1)
    low = lane < HD
    quarter = (lane % HD) < HD // 2

    def copy_to(src, dst, ss, rs, where):
        return pltpu.make_async_remote_copy(
            src_ref=src, dst_ref=dst, send_sem=ss, recv_sem=rs, device_id=where, device_id_type=MESH
        )

    def remote(src, dst, ss, rs, j):
        return copy_to(src, dst, ss, rs, dict(head=peer_of(h, j)))

    def across(src, dst, ss, rs):
        return copy_to(src, dst, ss, rs, dict(ctx=1 - c))

    def load(k, src, dst):
        return pltpu.make_async_copy(src, dst, r.in_sem.at[k])

    my_rows = pl.ds(pl.multiple_of(h * rows, rows), rows)
    my_pos = pl.ds(pl.multiple_of(c * half + h * rows, rows), rows)
    loads = SimpleNamespace(
        hid=load(0, r.hid.at[:, my_rows], hid_v),
        ga=load(1, r.ga, r.gains_v.at[0]),
        gf=load(11, r.gf, r.gains_v.at[1]),
        wk=load(3, r.wk, r.wk_v),
        wv=load(4, r.wv, r.wv_v),
        tab=load(5, r.tab.at[my_pos], r.tab_v.at[:, pl.ds(0, 128)]),
        wq=load(2, r.wq, r.wq_v),
        wo=load(6, r.wo, r.wo_v),
        wg=load(7, r.wg, wg_v),
        wu=load(8, r.wu, wu_v),
        wd=load(9, r.wd, wd_v),
        cot=load(10, r.cot, r.cot_v),
    )
    for cp in vars(loads).values():
        cp.start()

    plane = [(j, x) for j in range(HEADS) for x in range(2) if (j, x) != (0, 0)]

    def plane_id(j, x):
        return dict(head=peer_of(h, j), ctx=1 - c if x else c)

    barrier = pltpu.get_barrier_semaphore()
    for j, x in plane:
        pl.semaphore_signal(barrier, inc=1, device_id=plane_id(j, x), device_id_type=MESH)
    for k in range(1, nb):
        pl.semaphore_signal(barrier, inc=1, device_id=dict(batch=(z + k) % nb), device_id_type=MESH)
    pl.semaphore_wait(barrier, len(plane) + nb - 1)

    length = r.len[0]
    row_pos = c * half + h * rows + lax.broadcasted_iota(jnp.int32, (rows, 1), 0)
    valid = (row_pos < length).astype(F32)

    zero_w = jnp.zeros((rows, 128), F32)
    r.wide[...] = jnp.zeros(r.wide.shape, F32)
    vlo = r.wide.shape[1] // 2
    r.lse[0] = zero_w
    r.lse[1] = zero_w

    @pl.when(c == 0)
    def _():
        for p in range(2):
            r.kv[p, :, half:, :] = jnp.zeros((KV, half, 128), BF16)

    def fill_mask():
        for blk in range(2 * HEADS):
            own = blk < HEADS
            base = (c if own else 1 - c) * half + peer_of(h, blk % HEADS) * rows
            kp = base + lax.broadcasted_iota(jnp.int32, (rows, rows), 1)
            qp = c * half + h * rows + lax.broadcasted_iota(jnp.int32, (rows, rows), 0)
            ok = (kp <= qp) & (kp < length)
            r.bias[:, blk * rows : (blk + 1) * rows] = jnp.where(ok, 0.0, NEG)

    def fill_cotangent():
        for j in range(HEADS):
            pr = pl.ds(pl.multiple_of(peer_of(h, j) * rows, rows), rows)
            pos = c * half + peer_of(h, j) * rows + lax.broadcasted_iota(jnp.int32, (rows, 1), 0)
            ok = (pos < length).astype(F32)
            for b, lo, w in blocks(d):
                block = r.cot_v[lo : lo + w, pr].astype(F32).T * ok
                r.df[1, j, :, lo : lo + w] = block.astype(BF16)
                if j == 0:
                    r.d_res[:, lo : lo + w] = block

    def clear_sums():
        @pl.loop(0, 12)
        def _(i):
            r.gown[i] = jnp.zeros((cr, ff), F32)
            r.sf[i] = jnp.zeros((cr, ff), BF16)

        r.gain_v[...] = jnp.zeros((2, 1, d), F32)

    def share(k, e, j):
        return remote(r.psend.at[k, j - 1], r.precv.at[k, j - 1], r.p_ss.at[e, j], r.p_rs.at[e, j], j)

    def summed(k, e):
        total = r.part[k].astype(F32)
        for j in (1, 2, 3):
            share(k, e, j).wait_recv()
            total = total + r.precv[k, j - 1].astype(F32)
        return total

    def sent(k, e):
        for j in (1, 2, 3):
            share(k, e, j).wait_send()

    def rms(x, gain):
        inv = lax.rsqrt(jnp.mean(x * x, axis=-1, keepdims=True) + EPS)
        return x * inv * gain

    def turned(x):
        return jnp.where(quarter, -pltpu.roll(x, 128 - HD // 2, 1), pltpu.roll(x, HD // 2, 1))

    def rope(x):
        return x * r.tab_v[:, 0:128] + turned(x) * r.tab_v[:, 128:256]

    def unrope(x):
        return x * r.tab_v[:, 0:128] - turned(x) * r.tab_v[:, 128:256]

    def swap(x):
        return pltpu.roll(x, HD, 1)

    def blocks(width):
        return [(b, b * 128, min(128, width - b * 128)) for b in range(-(-width // 128))]

    def head_row(i):
        return i // GQ, (i % GQ) * rows

    def store_t(dst, src):
        for b, lo, w in blocks(d):
            dst[lo : lo + w, :] = src[:, lo : lo + w].T

    gain_a = lambda: r.gains_v[0]
    gain_f = lambda: r.gains_v[1]

    loads.tab.wait()
    both = r.tab_v[:, 0:128]
    r.tab_v[:, 128:256] = jnp.where(quarter, pltpu.roll(both, 128 - HD // 2, 1), both)
    r.tab_v[:, 0:128] = jnp.where(quarter, both, pltpu.roll(both, HD // 2, 1))
    loads.ga.wait()
    loads.gf.wait()
    loads.hid.wait()
    for b, lo, w in blocks(d):
        r.res[0, :, lo : lo + w] = hid_v[lo : lo + w, :].astype(F32).T

    def gather(e, src, dst, by_owner=False):
        def hop(k, ref, to, j):
            return remote(ref, to, r.ag_ss.at[e, k], r.ag_rs.at[e, k], j)

        at = (lambda j, near, x: dst(near, x)) if by_owner else (lambda j, near, x: dst(j, x))
        first = [hop(0, src(0), at(1, 0, 0), 1), hop(3, src(1), at(2, 0, 1), 2), hop(1, src(1), at(1, 0, 1), 1),
                 hop(2, src(0), at(2, 0, 0), 2)]
        relay = [hop(4, dst(1, 0), at(3, 1, 0), 2), hop(5, dst(2, 1), at(3, 2, 1), 1)]
        def start():
            for cp in first:
                cp.start()

        def hand_on():
            first[0].wait_recv()
            relay[0].start()
            first[1].wait_recv()
            relay[1].start()

        def wait(j):
            for cp in ((first[2],), (first[3],), relay)[j - 1]:
                cp.wait_recv()

        def drain():
            for cp in first + relay:
                cp.wait_send()

        return SimpleNamespace(start=start, hand_on=hand_on, wait=wait, drain=drain)

    def halves(ref):
        n = ref.shape[0] // 2
        return lambda x: ref.at[pl.ds(x * n, n)]

    @pl.loop(0, 2)
    def _(p):
        x = r.res[p]
        na = rms(x, gain_a()).astype(BF16)
        store_t(r.nat.at[p], na)

        @pl.when(p == 0)
        def _():
            loads.wk.wait()
            loads.wv.wait()

        r.wide[:, : KV * HD] = nt(na, r.wk_v[...])
        r.wide[:, vlo : vlo + KV * HD] = nt(na, r.wv_v[...])
        for b in range(-(-KV // 2)):
            kb = rope(r.wide[:, b * 128 : (b + 1) * 128])
            vb = r.wide[:, vlo + b * 128 : vlo + (b + 1) * 128]
            r.kv[p, 2 * b, 0:rows, :] = jnp.where(low, kb, swap(vb)).astype(BF16)
            if 2 * b + 1 < KV:
                r.kv[p, 2 * b + 1, 0:rows, :] = jnp.where(low, swap(kb), vb).astype(BF16)

        def to_peer(j, g):
            return remote(
                r.kv.at[p, g, pl.ds(0, rows)], r.kv.at[p, g, pl.ds(j * rows, rows)],
                r.kv_ss.at[p, g], r.kv_rs.at[p, g], j,
            )

        def to_partner(j, g):
            return across(
                r.kv.at[p, g, pl.ds(j * rows, rows)], r.kv.at[p, g, pl.ds(half + j * rows, rows)],
                r.kvc_ss.at[p, g], r.kvc_rs.at[p, g],
            )

        def all_peers(g):
            span = r.kv.at[p, g, pl.ds(rows, 3 * rows)]
            return remote(span, span, r.kv_ss.at[p, g], r.kv_rs.at[p, g], 1)

        def all_partner(g):
            span = r.kv.at[p, g, pl.ds(half, half)]
            return across(span, span, r.kvc_ss.at[p, g], r.kvc_rs.at[p, g])

        for g in range(KV):
            for j in (1, 2, 3):
                to_peer(j, g).start()

            @pl.when(c == 0)
            def _():
                to_partner(0, g).start()

        def arrive(g):
            all_peers(g).wait_recv()

            @pl.when(c == 0)
            def _():
                for j in (1, 2, 3):
                    to_partner(j, g).start()

        @pl.when(p == 0)
        def _():
            fill_mask()
            loads.wq.wait()

        r.wide[:, :d] = nn(na, r.wq_v[...])
        for b, lo, w in blocks(d):
            y = rope(r.wide[:, lo : lo + 128]).astype(BF16).astype(F32) * HD ** (-0.5)
            g, o = head_row(2 * b)
            r.ql[p, g, o : o + rows, :] = jnp.where(low, y, 0.0).astype(BF16)
            if 2 * b + 1 < QH:
                g, o = head_row(2 * b + 1)
                r.ql[p, g, o : o + rows, :] = jnp.where(low, swap(y), 0.0).astype(BF16)

        arrive(0)

        @pl.loop(0, KV)
        def _(g):
            @pl.when(g < KV - 1)
            def _():
                arrive(g + 1)

            @pl.when(c == 1)
            def _():
                all_partner(g).wait_recv()

            kv = r.kv[p, g]
            for k in range(GQ):
                s = nt(r.ql[p, g, k * rows : (k + 1) * rows, :], kv)
                s = jnp.where(r.bias[...] < 0.0, NEG, s)
                m = jnp.max(s, axis=-1, keepdims=True)
                e = jnp.exp(s - m)
                t = jnp.sum(e, axis=-1, keepdims=True)
                r.lse[p] += jnp.where(lane == g * GQ + k, m + jnp.log(t), 0.0)
                r.heads[g * GQ + k] = nn((e / t).astype(BF16), kv)

        mine = pl.ds(pl.multiple_of(p * rows, rows), rows)
        for g in range(KV):
            o0, o1, o2 = (r.heads[g * GQ + k] for k in range(GQ))
            r.aog[g, mine, 0:128] = jnp.where(low, 0.0, o0).astype(BF16)
            r.aog[g, mine, 128:256] = jnp.where(low, swap(o1), o2).astype(BF16)
        for b, lo, w in blocks(d):
            first = swap(r.heads[2 * b])
            both = jnp.where(low, first, r.heads[2 * b + 1]) if 2 * b + 1 < QH else first
            r.at[:, lo : lo + w] = both[:, :w].astype(BF16)

        @pl.when(p == 0)
        def _():
            loads.wo.wait()

        mid = r.res[p] + nn(r.at[...], r.wo_v[...])
        r.mid[p] = mid
        r.nf[p, 0] = rms(mid, gain_f()).astype(BF16)
        ag = gather(p, halves(r.nf.at[p, 0]), lambda j, x: halves(r.nf.at[p, j])(x))
        ag.start()

        @pl.when(p == 0)
        def _():
            loads.wg.wait()
            loads.wu.wait()
            loads.wd.wait()

        for j in range(HEADS):
            if j == 1:
                ag.hand_on()
            if j:
                ag.wait(j)
            nf = r.nf[p, j]
            gate = nn(nf, wg_v[...])
            up = nn(nf, wu_v[...])
            r.gate[p, j] = gate
            r.up[p, j] = up
            act = (gate / (1.0 + jnp.exp(-gate)) * up).astype(BF16)
            part = nt(act, wd_v[...])
            if j == 0:
                r.part[p] = part.astype(BF16)
            else:
                r.psend[p, j - 1] = part.astype(BF16)
                share(p, p, j).start()
        ag.drain()

        @pl.when(p == 0)
        def _():
            loads.cot.wait()
            fill_cotangent()
            clear_sums()
            r.res[1] = valid * (r.mid[0] + summed(0, 0))
            sent(0, 0)

        @pl.loop(0, KV)
        def _(g):
            all_peers(g).wait_send()

            @pl.when(c == 0)
            def _():
                all_partner(g).wait_send()

    def final(k, out):
        def there(j, x):
            at = pl.ds(pl.multiple_of(peer_of(h, j) * rows, rows), rows)
            return out.at[pl.ds(x * hd2, hd2), at]

        own = pltpu.make_async_copy(r.fin.at[k], out.at[:, my_rows], r.loc_sem.at[k])
        ag = gather(3 + k, halves(r.fin.at[k]), there, True)

        def send(value):
            store_t(r.fin.at[k], value.astype(BF16))
            own.start()
            ag.start()

        return SimpleNamespace(send=send, own=own, hand_on=ag.hand_on, wait=ag.wait, drain=ag.drain)

    low_side = z < nb // 2
    middle = (z == nb // 2 - 1) | (z == nb // 2)
    handed = (z > 0) & (z < nb - 1)
    inwards = jnp.where(low_side, 1, -1)

    def zcopy(src, dst, ss, rs, dz):
        return copy_to(src, dst, ss, rs, dict(batch=z + dz))

    def to_next(i):
        return zcopy(r.zs.at[i], r.zu.at[i], r.z_s0.at[i], r.z_ur.at[i], inwards)

    def to_middle(i):
        return zcopy(r.zs.at[i], r.zb.at[i], r.z_s0.at[i], r.z_br.at[i], inwards)

    def to_outer(i, src):
        return zcopy(src.at[i], r.zb.at[i], r.z_s1.at[i], r.z_br.at[i], -inwards)

    def inward(i, own):
        @pl.when(handed)
        def _():
            to_next(i).wait_recv()
            r.zs[i] = (own() + r.zu[i].astype(F32)).astype(BF16)

        @pl.when(jnp.logical_not(handed))
        def _():
            r.zs[i] = own().astype(BF16)

        @pl.when(middle)
        def _():
            to_middle(i).start()

        @pl.when(jnp.logical_not(middle))
        def _():
            to_next(i).start()

    def og_local(i, src):
        return pltpu.make_async_copy(src.at[i], r.og.at[i // 4, c, i % 4], r.og_loc.at[i])

    def og_across(i, src):
        return across(src.at[i], r.og.at[i // 4, c, i % 4], r.og_ss.at[i], r.og_rs.at[i])

    def ex_local(q, src):
        return pltpu.make_async_copy(src.at[12 + q, :, pl.ds(512, 128)], r.ex.at[h, c, q], r.ex_loc.at[q])

    def ex_plane(q, src, j, x):
        return copy_to(
            src.at[12 + q, :, pl.ds(512, 128)], r.ex.at[h, c, q],
            r.ex_ss.at[q, 2 * j + x], r.ex_rs.at[q, 2 * j + x], plane_id(j, x),
        )

    def outward(i):
        def place(src):
            @pl.when(handed)
            def _():
                to_outer(i, src).start()

            og_local(i, src).start()
            og_across(i, src).start()
            if isinstance(i, int) and i >= 12:
                ex_local(i - 12, src).start()
                for j, x in plane:
                    ex_plane(i - 12, src, j, x).start()

        to_middle(i).wait_recv()

        @pl.when(middle)
        def _():
            to_middle(i).wait_send()
            r.zs[i] = (r.zs[i].astype(F32) + r.zb[i].astype(F32)).astype(BF16)
            place(r.zs)

        @pl.when(jnp.logical_not(middle))
        def _():
            place(r.zb)

    def ffn_half(t):
        sl = pl.ds(4 * t, 4)
        return across(r.sf.at[sl], r.rf.at[sl], r.f_ss.at[t], r.f_rs.at[t])

    def ffn_piece(i):
        @pl.when(i % 4 == 0)
        def _():
            ffn_half(i // 4).wait_recv()

        inward(i, lambda: r.gown[i] + r.rf[i].astype(F32))

    def within(i, cond, do):
        if isinstance(i, int) and not 0 <= i < 16:
            return

        @pl.when((i >= 0) & (i < 16) & cond)
        def _():
            do(i)

    def slot(k):
        piece = lambda i: (attention_piece if isinstance(i, int) and i >= 12 else ffn_piece)(i)
        within(k, jnp.logical_not(handed), piece)
        within(k - 2, handed, piece)
        within(k - 4, middle, outward)
        within(k - 6, jnp.logical_not(middle), outward)

    def norm_bwd(x, gain, dn):
        inv = lax.rsqrt(jnp.mean(x * x, axis=-1, keepdims=True) + EPS)
        u = gain * dn
        dx = inv * u - x * (inv * inv * inv) * jnp.mean(x * u, axis=-1, keepdims=True)
        return dx, jnp.sum(dn * x * inv, axis=0, keepdims=True)

    mine_half = pl.ds(pl.multiple_of(c * hd2, hd2), hd2)
    other_half = pl.ds(pl.multiple_of((1 - c) * hd2, hd2), hd2)

    def a_half(g):
        src = r.wf.at[pl.ds(pl.multiple_of(g * hd2, hd2), hd2), pl.ds(0, 512)]
        return across(src, r.ra.at[g], r.a_ss.at[g], r.a_rs.at[g])

    def first_group(to):
        g = jnp.int32(KV - 1)
        for k in reversed(range(KV - 1)):
            g = jnp.where(r.own[k] == to, k, g)
        return g

    g1 = jnp.int32(0)
    for k in range(1, KV):
        for i in range(k):
            g1 = jnp.where(r.own[k] == r.own[i], k, g1)

    def own_share(to, q):
        at = pl.ds(q * cr, cr)
        g0 = first_group(to)
        first = r.ha[g0, at, :].astype(F32) + r.ra[g0, at, :].astype(F32)
        cols = pl.ds(pl.multiple_of(to * 128, 128), 128)
        second = r.ha[g1, at, cols].astype(F32) + r.ra[g1, at, cols].astype(F32)
        return jnp.concatenate([first, second], axis=1)

    def head_share(j, q):
        i = 4 * (j - 1) + q
        return remote(r.sf.at[i], r.rf2.at[i], r.h_ss.at[j, q], r.h_rs.at[j, q], j)

    def attention_sums():
        @pl.loop(0, KV)
        def _(g):
            def product(rows_of):
                first = nn(jnp.concatenate([r.nat[0, rows_of, :], r.nat[1, rows_of, :]], axis=1), r.dpg[g])
                second = nn(jnp.concatenate([r.dat[0, rows_of, :], r.dat[1, rows_of, :]], axis=1), r.aog[g])
                return first[:, :256], first[:, 256:] + second[:, :128], second[:, 128:]

            def put(dst, parts):
                dst[:, 0:256] = parts[0].astype(BF16)
                dst[:, 256:384] = parts[1].astype(BF16)
                dst[:, 384:512] = parts[2].astype(BF16)

            put(r.wf.at[pl.ds(pl.multiple_of(g * hd2, hd2), hd2)], product(other_half))
            a_half(g).start()
            put(r.ha.at[g], product(mine_half))
            slot(KV + 1 + g)

        @pl.loop(0, KV)
        def _(g):
            a_half(g).wait_recv()

        for t in range(3):
            ffn_half(t).wait_send()
        for q in range(4):
            for j in (3, 1, 2):
                r.sf[4 * (j - 1) + q] = own_share(peer_of(h, j), q).astype(BF16)
                head_share(j, q).start()

    def attention_piece(i):
        q = i - 12

        def own():
            v = own_share(h, q)
            for j in (1, 2, 3):
                head_share(j, q).wait_recv()
                v = v + r.rf2[4 * (j - 1) + q].astype(F32)
            return v

        inward(i, own)

    @pl.loop(0, 2)
    def _(turn):
        p = 1 - turn
        ag = gather(2, halves(r.df.at[0, 0]), lambda j, x: halves(r.df.at[0, j])(x))

        @pl.when(p == 0)
        def _():
            block = r.d_res[...] * valid
            r.d_res[...] = block
            r.df[0, 0] = block.astype(BF16)
            ag.start()

        for j in range(HEADS):
            if j:
                @pl.when(p == 0)
                def _():
                    if j == 1:
                        ag.hand_on()
                    ag.wait(j)

            d_act = nn(r.df[p, j], wd_v[...])
            gate, up = r.gate[p, j], r.up[p, j]
            s = 1.0 / (1.0 + jnp.exp(-gate))
            dg = (d_act * up * s * (1.0 + gate * (1.0 - s))).astype(BF16)
            du = (d_act * (gate * s)).astype(BF16)
            r.act[j] = (gate * s * up).astype(BF16)
            r.dg[j] = dg
            r.du[j] = du
            part = nt(dg, wg_v[...]) + nt(du, wu_v[...])
            if j == 0:
                r.part[1 - p] = part.astype(BF16)
            else:
                r.psend[1 - p, j - 1] = part.astype(BF16)
                share(1 - p, 3 - p, j).start()
        for t, rhs in ((0, r.dg), (1, r.du), (2, r.act)):
            if t != 1:
                src = r.nf if t == 0 else r.df
                for j in range(HEADS):
                    store_t(lhs.at[:, j * rows : (j + 1) * rows], src[p, j])
            right = rhs[...].reshape(half, ff)
            theirs = nn(lhs[other_half, :], right)
            for q in range(4):
                v = theirs[q * cr : (q + 1) * cr] + r.sf[4 * t + q].astype(F32)
                r.sf[4 * t + q] = v.astype(BF16)

            @pl.when(p == 0)
            def _():
                ffn_half(t).start()

            ours = nn(lhs[mine_half, :], right)
            for q in range(4):
                r.gown[4 * t + q] += ours[q * cr : (q + 1) * cr]

        @pl.when(p == 1)
        def _():
            final(0, r.out).send(valid * (r.mid[1] + summed(1, 1)))
            sent(1, 1)

        dn = summed(1 - p, 3 - p)
        dx, dgain = norm_bwd(r.mid[p], gain_f(), dn)
        d_mid = r.d_res[...] + dx
        r.d_mid[...] = d_mid
        r.gain_v[1] += dgain
        da = d_mid.astype(BF16)
        store_t(r.dat.at[p], da)
        r.wide[:, :d] = nt(da, r.wo_v[...])
        for b, lo, w in blocks(d):
            y = r.wide[:, lo : lo + 128]
            g, o = head_row(2 * b)
            r.ou[g, o : o + rows, :] = jnp.where(low, 0.0, swap(y)).astype(BF16)
            if 2 * b + 1 < QH:
                g, o = head_row(2 * b + 1)
                r.ou[g, o : o + rows, :] = jnp.where(low, 0.0, y).astype(BF16)

        def hop(g):
            return across(r.dkv_ctx.at[g], r.dkv_ctx_r.at[p, g], r.dc_ss.at[p, g], r.dc_rs.at[p, g])

        def to_owner(j, g):
            return remote(
                r.dkv_s.at[g, j - 1], r.dkv_r.at[g, j - 1], r.dkv_ss.at[p, g], r.dkv_rs.at[p, g], j
            )

        def all_owners(g):
            return remote(r.dkv_s.at[g], r.dkv_r.at[g], r.dkv_ss.at[p, g], r.dkv_rs.at[p, g], 1)

        def pass_on(g):
            @pl.when(c == 0)
            def _():
                hop(g).wait_recv()
                r.dkv[g] += r.dkv_ctx_r[p, g].astype(F32)

            for j in (1, 2, 3):
                r.dkv_s[g, j - 1] = r.dkv[g, :, j * rows : (j + 1) * rows].astype(BF16)
                to_owner(j, g).start()

        @pl.loop(0, KV)
        def _(g):
            kv = r.kv[p, g]
            acc = None
            for k in range(GQ):
                q = r.ql[p, g, k * rows : (k + 1) * rows, :]
                o = r.ou[g, k * rows : (k + 1) * rows, :]
                s = nt(q, kv)
                s = jnp.where(r.bias[...] < 0.0, NEG, s)
                lse = jnp.sum(jnp.where(lane == g * GQ + k, r.lse[p], 0.0), axis=-1, keepdims=True)
                pr = jnp.exp(s - lse)
                dpr = nt(o, kv)
                delta = jnp.sum(pr * dpr, axis=-1, keepdims=True)
                ds = (pr * (dpr - delta)).astype(BF16)
                r.heads[g * GQ + k] = unrope(nn(ds, kv) * HD ** (-0.5))
                t = nn(o.T, pr.astype(BF16)) + nn(q.T, ds)
                acc = t if acc is None else acc + t
            r.dkv[g] = acc[:, :half]
            r.dkv_ctx[g] = acc[:, half:].astype(BF16)

            @pl.when(c == 1)
            def _():
                hop(g).start()

            @pl.when(g > 0)
            def _():
                pass_on(g - 1)

            @pl.when(p == 0)
            def _():
                slot(g)

        pass_on(KV - 1)
        mine = pl.ds(pl.multiple_of(p * rows, rows), rows)
        for b, lo, w in blocks(d):
            y = r.heads[2 * b]
            if 2 * b + 1 < QH:
                y = jnp.where(low, y, swap(r.heads[2 * b + 1]))
            r.at[:, lo : lo + w] = y[:, :w].astype(BF16)
        for g in range(KV):
            both = jnp.where(low, r.heads[g * GQ], swap(r.heads[g * GQ + 1]))
            r.dpg[g, mine, 0:128] = both.astype(BF16)

        r.wide[:, :d] = nt(r.at[...], r.wq_v[...])

        @pl.when(p == 0)
        def _():
            slot(KV)

        keys, vals = [], []
        for g in range(KV):
            t = r.dkv[g, :, 0:rows]
            all_owners(g).wait_recv()
            for j in range(3):
                t = t + r.dkv_r[g, j].astype(F32)
            t = t.T
            kt, vt = unrope(t), swap(t)
            keys.append(kt)
            vals.append(t)
            r.dpg[g, mine, 128:256] = jnp.where(low, r.heads[g * GQ + 2], swap(kt)).astype(BF16)
            r.dpg[g, mine, 256:384] = jnp.where(low, vt, 0.0).astype(BF16)
        for b, lo, w in blocks(KV * HD):
            kb, vb = keys[2 * b], swap(vals[2 * b])
            if 2 * b + 1 < KV:
                kb = jnp.where(low, kb, swap(keys[2 * b + 1]))
                vb = jnp.where(low, vb, vals[2 * b + 1])
            r.dk[:, lo : lo + w] = kb[:, :w].astype(BF16)
            r.dv[:, lo : lo + w] = vb[:, :w].astype(BF16)
        @pl.when(p == 0)
        def _():
            attention_sums()

        dna = r.wide[:, :d] + nn(r.dk[...], r.wk_v[...]) + nn(r.dv[...], r.wv_v[...])
        dx, dgain = norm_bwd(r.res[p], gain_a(), dna)
        r.d_res[...] = r.d_mid[...] + dx
        r.gain_v[0] += dgain
        sent(1 - p, 3 - p)

        @pl.when(p == 0)
        def _():
            ag.drain()

        @pl.when(p == 1)
        def _():
            final(0, r.out).hand_on()


        @pl.loop(0, KV)
        def _(g):
            all_owners(g).wait_send()

            @pl.when(c == 1)
            def _():
                hop(g).wait_send()

    final(1, r.gin).send(r.d_res[...])

    me = 2 * h + c
    r.gain_p[me] = r.gain_v[...]
    gp = [copy_to(r.gain_p.at[me], r.gain_p.at[me], r.gp_ss.at[2 * j + x], r.gp_rs.at[2 * j + x], plane_id(j, x))
          for j, x in plane]
    for cp in gp:
        cp.start()

    for cp in gp:
        cp.wait_recv()
    total = r.gain_p[0]
    for k in range(1, 2 * HEADS):
        total = total + r.gain_p[k]
    r.gain_z[z] = total
    gz = [copy_to(r.gain_z.at[z], r.gain_z.at[z], r.gz_ss.at[k], r.gz_rs.at[k], dict(batch=(z + k) % nb))
          for k in range(1, nb)]
    for cp in gz:
        cp.start()

    for k in range(2 * KV + 1, 22):
        slot(k)
        if k == 2 * KV + 1:
            final(1, r.gin).hand_on()

    for cp in gz:
        cp.wait_recv()
    total = r.gain_z[0]
    for k in range(1, nb):
        total = total + r.gain_z[k]
    r.gain_v[...] = total
    gains_out = pltpu.make_async_copy(r.gain_v, r.gains_out, r.loc_sem.at[2])
    gains_out.start()

    gains_out.wait()
    for cp in gp + gz:
        cp.wait_send()
    for j in (1, 2, 3):
        for q in range(4):
            head_share(j, q).wait_send()

    @pl.loop(0, KV)
    def _(g):
        a_half(g).wait_send()

    @pl.loop(0, 16)
    def _(i):
        og_local(i, r.zs).wait()
        og_across(i, r.zs).wait_send()
        og_across(i, r.zs).wait_recv()

        @pl.when(jnp.logical_not(middle))
        def _():
            to_next(i).wait_send()

        @pl.when(handed)
        def _():
            to_outer(i, r.zs).wait_send()

    for q in range(4):
        ex_local(q, r.zs).wait()
        for j, x in plane:
            ex_plane(q, r.zs, j, x).wait_send()
            ex_plane(q, r.zs, j, x).wait_recv()
    for k, out in ((0, r.out), (1, r.gin)):
        end = final(k, out)
        end.own.wait()
        for j in (1, 2, 3):
            end.wait(j)
        end.drain()


def put_kernel(own, o, gin, og, ex, ga, gf, o_out, gin_out, gq, gk, gv, go, gg, gu, gd, ga_out, gf_out):
    h = lax.axis_index("head")
    held = jnp.int32(0)
    for k in range(KV):
        held = held + jnp.where(own[k] == h, 1, 0)
    gw = GQ * HD
    o_out[...] = o[...]
    gin_out[...] = gin[...].astype(F32)
    gg[...] = og[0].astype(F32)
    gu[...] = og[1].astype(F32)
    gd[...] = og[2].astype(F32)
    ga_out[...] = ga[...]
    gf_out[...] = gf[...]
    first = og[3, :, 0:512].astype(F32)
    second = jnp.concatenate([ex[k].astype(F32) for k in range(HEADS)], axis=1)
    second = jnp.where(held > 1, second, 0.0)
    for out, lo, width in ((gq, 0, gw), (gk, gw, HD), (gv, gw + HD, HD), (go, gw + 2 * HD, gw)):
        out[...] = jnp.concatenate([first[:, lo : lo + width], second[:, lo : lo + width]], axis=1)


def body(nb, hidden_in, cotangent, lengths, owners, w_query, w_key, w_value, w_output, gate_weight, up_weight, down_weight,
         gain_attn, gain_ffn):
    half, d = hidden_in.shape[1:]
    ff = gate_weight.shape[1]
    rows = half // HEADS
    cr = d // 8
    scratch = scratch_of(rows, d, ff, nb)
    anyspec = pl.BlockSpec(memory_space=pl.ANY)
    smem = pl.BlockSpec(memory_space=pltpu.SMEM)
    sd = jax.ShapeDtypeStruct
    ins = dict(
        hid=anyspec, cot=anyspec, len=smem, own=smem, ga=anyspec, gf=anyspec, tab=anyspec,
        wq=anyspec, wk=anyspec, wv=anyspec, wo=anyspec, wg=anyspec, wu=anyspec, wd=anyspec,
    )
    outs = dict(
        out=sd((d, half), BF16), gin=sd((d, half), BF16),
        og=sd((4, 2, 4, cr, ff), BF16), ex=sd((HEADS, 2, 4, cr, 128), BF16), gains_out=sd((2, 1, d), F32),
    )
    names = tuple(ins) + tuple(outs) + tuple(scratch)
    o, gin, og, ex, gains = pl.pallas_call(
        functools.partial(step_kernel, names, rows, d, ff, nb),
        out_shape=tuple(outs.values()),
        in_specs=list(ins.values()),
        out_specs=(anyspec,) * len(outs),
        scratch_shapes=list(scratch.values()),
        compiler_params=pltpu.CompilerParams(
            collective_id=0, has_side_effects=True, vmem_limit_bytes=67043328
        ),
    )(
        hidden_in[0].T, cotangent[0].T, lengths, owners, gain_attn[None], gain_ffn[None],
        jnp.asarray(rope_table(2 * half)), w_query, w_key.T, w_value.T, w_output, gate_weight, up_weight, down_weight.T,
    )
    gw, block = GQ * HD, lambda *shape: (lambda index: pl.BlockSpec(shape, index))
    rowwise = lambda width: block(cr, width)(lambda i: (i, 0))
    gains_spec = lambda k: block(None, 1, d)(lambda i: (k, 0, 0))
    gain_out = block(1, d)(lambda i: (0, 0))
    o, gin, gq, gk, gv, go, gg, gu, gd, ga, gf = pl.pallas_call(
        put_kernel,
        grid=(8,),
        out_shape=(
            sd((d, half), BF16), sd((d, half), F32), sd((d, 2 * gw), F32), sd((d, 2 * HD), F32), sd((d, 2 * HD), F32),
            sd((d, 2 * gw), F32), sd((d, ff), F32), sd((d, ff), F32), sd((d, ff), F32), sd((1, d), F32), sd((1, d), F32),
        ),
        in_specs=[
            smem, rowwise(half), rowwise(half), block(4, None, None, cr, ff)(lambda i: (0, i // 4, i % 4, 0, 0)),
            block(HEADS, None, None, cr, 128)(lambda i: (0, i // 4, i % 4, 0, 0)), gains_spec(0), gains_spec(1),
        ],
        out_specs=(
            rowwise(half), rowwise(half), rowwise(2 * gw), rowwise(2 * HD), rowwise(2 * HD), rowwise(2 * gw),
            rowwise(ff), rowwise(ff), rowwise(ff), gain_out, gain_out,
        ),
    )(owners, o, gin, og, ex, gains, gains)
    return o.T[None], gin.T[None], gq, gk, gv, go.T, gg, gu, gd.T, ga[0], gf[0]


def solution(mesh):
    rep = P()
    io = P("batch", "ctx", None)
    in_specs = (io, io, P("batch"), rep, rep, rep, rep, rep, P(None, "head"), P(None, "head"), P("head", None), rep, rep)
    out_specs = (io, io, P(None, "head"), P(None, "head"), P(None, "head"), P("head", None), P(None, "head"),
                 P(None, "head"), P("head", None), rep, rep)
    return jax.shard_map(
        functools.partial(body, mesh.shape["batch"]), mesh=mesh, in_specs=in_specs, out_specs=out_specs, check_vma=False
    )
```

profile of v0, /device:TPU:27, one launch (start us, length us, event | category | flops | bytes accessed | tf_op | source)
XLA Modules:
  0.0 249.6 jit_solution(12984831083985216627)
XLA Ops:
  1.3 238.3 %shard_map.221 = (bf16[960,512]{1,0:T(8,128)(2,1)}, bf16[960,512]{1,0:T(8,128)(2,1)}, bf16[4,2,4,120,640]{4,3,2,1,0:T(8,128)(2,1)}, bf16[4,2,4,120,128]{4,3,2,1,0:T(8,128)(2,1)}, f32[2,1,960]{2,1,0:T(1,128)}) custom-call(bf16[960,512]{1,0:T(8,128)(2,1)} %bitcast.22, bf16[960,512]{1,0:T(8,128)(2,1)} %bitcast.23, s32[1]{0:T(128)S(6)} %copy.25.refs_2_, s32[5]{0:T(128)} %own.1, ...), custom_call_target="tpu_custom_call" | custom-call | tf_op jit(solution)/shard_map/pallas_call | solution.py:982
  239.6 9.8 %shard_map.222 = (bf16[960,512]{1,0:T(8,128)(2,1)}, f32[960,512]{1,0:T(8,128)}, f32[960,384]{1,0:T(8,128)}, f32[960,128]{1,0:T(8,128)}, f32[960,128]{1,0:T(8,128...) custom-call(s32[5]{0:T(128)} %own.1, ...), custom_call_target="tpu_custom_call" | custom-call | tf_op jit(solution)/shard_map/pallas_call | solution.py:999
where the time goes:
time: 253 us; the launch traced here: 250 us
  Pallas kernels  248 us (98%)
    pallas_call x1, Pallas kernels, body(): pl.pallas_call(functools.partial(step_kernel, names, rows, d, ff, nb), ou...  238 us
    pallas_call x1, Pallas kernels, body(): pl.pallas_call(put_kernel, grid=(8,), out_shape=(sd((d, half), BF16), sd(...  9.84 us

commit v1 on v0

--- a/solution.py
+++ b/solution.py
@@ -493,12 +493,11 @@
         own = pltpu.make_async_copy(r.fin.at[k], out.at[:, my_rows], r.loc_sem.at[k])
         ag = gather(3 + k, halves(r.fin.at[k]), there, True)
 
-        def send(value):
+        def put(value):
             store_t(r.fin.at[k], value.astype(BF16))
             own.start()
-            ag.start()
-
-        return SimpleNamespace(send=send, own=own, hand_on=ag.hand_on, wait=ag.wait, drain=ag.drain)
+
+        return SimpleNamespace(put=put, own=own, send=ag.start, hand_on=ag.hand_on, wait=ag.wait, drain=ag.drain)
 
     low_side = z < nb // 2
     middle = (z == nb // 2 - 1) | (z == nb // 2)
@@ -550,6 +549,16 @@
             r.ex_ss.at[q, 2 * j + x], r.ex_rs.at[q, 2 * j + x], plane_id(j, x),
         )
 
+    def ex_hand_on(q, j):
+        at = r.ex.at[peer_of(h, j), c, q]
+        return across(at, at, r.ex_ss.at[q, 2 * j + 1], r.ex_rs.at[q, 2 * j + 1])
+
+    def ex_arrive(q):
+        for j in (1, 2, 3):
+            ex_plane(q, r.zs, j, 0).wait_send()
+            ex_plane(q, r.zs, j, 0).wait_recv()
+            ex_hand_on(q, j).start()
+
     def outward(i):
         def place(src):
             @pl.when(handed)
@@ -560,7 +569,7 @@
             og_across(i, src).start()
             if isinstance(i, int) and i >= 12:
                 ex_local(i - 12, src).start()
-                for j, x in plane:
+                for j, x in ((3, 0), (1, 0), (2, 0), (0, 1)):
                     ex_plane(i - 12, src, j, x).start()
 
         to_middle(i).wait_recv()
@@ -594,12 +603,23 @@
         def _():
             do(i)
 
-    def slot(k):
+    outer = jnp.logical_not(handed)
+
+    def outer_pieces(lo, hi):
+        @pl.when(outer)
+        def _():
+            pl.loop(lo, hi)(ffn_piece)
+
+    def turn(m):
         piece = lambda i: (attention_piece if isinstance(i, int) and i >= 12 else ffn_piece)(i)
-        within(k, jnp.logical_not(handed), piece)
-        within(k - 2, handed, piece)
-        within(k - 4, middle, outward)
-        within(k - 6, jnp.logical_not(middle), outward)
+        within(m, handed, piece)
+        if isinstance(m, int) and m in (9, 11, 13, 15):
+            within(12 + (m - 9) // 2, outer, piece)
+        if not isinstance(m, int) or m <= 13:
+            within(m - 2, middle, outward)
+        if isinstance(m, int) and m >= 13:
+            within(m - 1, middle, outward)
+        within(m - 5, jnp.logical_not(middle), outward)
 
     def norm_bwd(x, gain, dn):
         inv = lax.rsqrt(jnp.mean(x * x, axis=-1, keepdims=True) + EPS)
@@ -653,7 +673,10 @@
             put(r.wf.at[pl.ds(pl.multiple_of(g * hd2, hd2), hd2)], product(other_half))
             a_half(g).start()
             put(r.ha.at[g], product(mine_half))
-            slot(KV + 1 + g)
+
+            @pl.when(g % 3 == 1)
+            def _():
+                turn(KV + g // 3)
 
         @pl.loop(0, KV)
         def _(g):
@@ -665,6 +688,7 @@
             for j in (3, 1, 2):
                 r.sf[4 * (j - 1) + q] = own_share(peer_of(h, j), q).astype(BF16)
                 head_share(j, q).start()
+        turn(KV + 2)
 
     def attention_piece(i):
         q = i - 12
@@ -679,8 +703,8 @@
         inward(i, own)
 
     @pl.loop(0, 2)
-    def _(turn):
-        p = 1 - turn
+    def _(back):
+        p = 1 - back
         ag = gather(2, halves(r.df.at[0, 0]), lambda j, x: halves(r.df.at[0, j])(x))
 
         @pl.when(p == 0)
@@ -731,9 +755,14 @@
             for q in range(4):
                 r.gown[4 * t + q] += ours[q * cr : (q + 1) * cr]
 
+        @pl.when(p == 0)
+        def _():
+            outer_pieces(0, 8)
+
         @pl.when(p == 1)
         def _():
-            final(0, r.out).send(valid * (r.mid[1] + summed(1, 1)))
+            final(0, r.out).put(valid * (r.mid[1] + summed(1, 1)))
+            final(0, r.out).send()
             sent(1, 1)
 
         dn = summed(1 - p, 3 - p)
@@ -801,9 +830,13 @@
             def _():
                 pass_on(g - 1)
 
-            @pl.when(p == 0)
-            def _():
-                slot(g)
+            @pl.when((p == 0) & (g == 0))
+            def _():
+                outer_pieces(8, 12)
+
+            @pl.when((p == 0) & (g > 0))
+            def _():
+                turn(g - 1)
 
         pass_on(KV - 1)
         mine = pl.ds(pl.multiple_of(p * rows, rows), rows)
@@ -820,7 +853,7 @@
 
         @pl.when(p == 0)
         def _():
-            slot(KV)
+            turn(KV - 1)
 
         keys, vals = [], []
         for g in range(KV):
@@ -868,7 +901,7 @@
             def _():
                 hop(g).wait_send()
 
-    final(1, r.gin).send(r.d_res[...])
+    final(1, r.gin).put(r.d_res[...])
 
     me = 2 * h + c
     r.gain_p[me] = r.gain_v[...]
@@ -888,9 +921,11 @@
     for cp in gz:
         cp.start()
 
-    for k in range(2 * KV + 1, 22):
-        slot(k)
-        if k == 2 * KV + 1:
+    for m in range(KV + 3, 21):
+        turn(m)
+        if m == 15:
+            final(1, r.gin).send()
+        if m == 18:
             final(1, r.gin).hand_on()
 
     for cp in gz:
@@ -902,6 +937,9 @@
     gains_out = pltpu.make_async_copy(r.gain_v, r.gains_out, r.loc_sem.at[2])
     gains_out.start()
 
+    for q in range(4):
+        ex_arrive(q)
+
     gains_out.wait()
     for cp in gp + gz:
         cp.wait_send()
@@ -929,9 +967,9 @@
 
     for q in range(4):
         ex_local(q, r.zs).wait()
-        for j, x in plane:
-            ex_plane(q, r.zs, j, x).wait_send()
-            ex_plane(q, r.zs, j, x).wait_recv()
+        ex_plane(q, r.zs, 0, 1).wait()
+        for j in (1, 2, 3):
+            ex_hand_on(q, j).wait()
     for k, out in ((0, r.out), (1, r.gin)):
         end = final(k, out)
         end.own.wait()

time: 253 us -> 242 us (0.957)
  Pallas kernels: 248 us -> 238 us
    pallas_call x1, Pallas kernels: 238 us -> 228 us  [body(): pl.pallas_call(functools.partial(step_kernel, names, rows, d, ff, nb), ou...]
where the time goes in v1:
time: 242 us; the launch traced here: 239 us
  Pallas kernels  238 us (98%)
    pallas_call x1, Pallas kernels, body(): pl.pallas_call(functools.partial(step_kernel, names, rows, d, ff, nb), ou...  228 us
    pallas_call x1, Pallas kernels, body(): pl.pallas_call(put_kernel, grid=(8,), out_shape=(sd((d, half), BF16), sd(...  9.84 us

profile of v1, /device:TPU:27, one launch (start us, length us, event | category | flops | bytes accessed | tf_op | source)
XLA Modules:
  0.0 239.0 jit_solution(4352571522105699517)
XLA Ops:
  1.3 227.7 %shard_map.221 = (bf16[960,512]{1,0:T(8,128)(2,1)}, bf16[960,512]{1,0:T(8,128)(2,1)}, bf16[4,2,4,120,640]{4,3,2,1,0:T(8,128)(2,1)}, bf16[4,2,4,120,128]{4,3,2,1,0:T(8,128)(2,1)}, f32[2,1,960]{2,1,0:T(1,128)}) custom-call(bf16[960,512]{1,0:T(8,128)(2,1)} %bitcast.22, bf16[960,512]{1,0:T(8,128)(2,1)} %bitcast.23, s32[1]{0:T(128)S(6)} %copy.25.refs_2_, s32[5]{0:T(128)} %own.1, ...), custom_call_target="tpu_custom_call" | custom-call | tf_op jit(solution)/shard_map/pallas_call | solution.py:1020
  229.0 9.8 %shard_map.222 = (bf16[960,512]{1,0:T(8,128)(2,1)}, f32[960,512]{1,0:T(8,128)}, f32[960,384]{1,0:T(8,128)}, f32[960,128]{1,0:T(8,128)}, f32[960,128]{1,0:T(8,128...) custom-call(s32[5]{0:T(128)} %own.1, ...), custom_call_target="tpu_custom_call" | custom-call | tf_op jit(solution)/shard_map/pallas_call | solution.py:1037

commit v2 on v1

--- a/solution.py
+++ b/solution.py
@@ -124,17 +124,17 @@
         dkv_rs=dma((2, KV)),
         f_ss=dma((3,)),
         f_rs=dma((3,)),
-        z_s0=dma((16,)),
-        z_s1=dma((16,)),
-        z_ur=dma((16,)),
-        z_br=dma((16,)),
-        og_loc=dma((16,)),
-        og_ss=dma((16,)),
-        og_rs=dma((16,)),
+        z_s0=dma((17,)),
+        z_s1=dma((17,)),
+        z_ur=dma((17,)),
+        z_br=dma((17,)),
+        og_loc=dma((17,)),
+        og_ss=dma((17,)),
+        og_rs=dma((17,)),
         a_ss=dma((KV,)),
         a_rs=dma((KV,)),
-        h_ss=dma((4, 4)),
-        h_rs=dma((4, 4)),
+        h_ss=dma((4, 5)),
+        h_rs=dma((4, 5)),
         ex_loc=dma((4,)),
         ex_ss=dma((4, 8)),
         ex_rs=dma((4, 8)),
@@ -417,12 +417,12 @@
             kv = r.kv[p, g]
             for k in range(GQ):
                 s = nt(r.ql[p, g, k * rows : (k + 1) * rows, :], kv)
-                s = jnp.where(r.bias[...] < 0.0, NEG, s)
+                s = s + r.bias[...]
                 m = jnp.max(s, axis=-1, keepdims=True)
                 e = jnp.exp(s - m)
                 t = jnp.sum(e, axis=-1, keepdims=True)
                 r.lse[p] += jnp.where(lane == g * GQ + k, m + jnp.log(t), 0.0)
-                r.heads[g * GQ + k] = nn((e / t).astype(BF16), kv)
+                r.heads[g * GQ + k] = nn((e * (1.0 / t)).astype(BF16), kv)
 
         mine = pl.ds(pl.multiple_of(p * rows, rows), rows)
         for g in range(KV):
@@ -507,24 +507,34 @@
     def zcopy(src, dst, ss, rs, dz):
         return copy_to(src, dst, ss, rs, dict(batch=z + dz))
 
+    def columns(i):
+        return {15: (384, ff - 384), 16: (0, 384)}.get(i, (0, ff)) if isinstance(i, int) else (0, ff)
+
+    def place(i):
+        return min(i, 15) if isinstance(i, int) else i
+
+    def view(ref, i):
+        lo, n = columns(i)
+        return ref.at[i] if n == ff else ref.at[place(i), :, pl.ds(lo, n)]
+
     def to_next(i):
-        return zcopy(r.zs.at[i], r.zu.at[i], r.z_s0.at[i], r.z_ur.at[i], inwards)
+        return zcopy(view(r.zs, i), view(r.zu, i), r.z_s0.at[i], r.z_ur.at[i], inwards)
 
     def to_middle(i):
-        return zcopy(r.zs.at[i], r.zb.at[i], r.z_s0.at[i], r.z_br.at[i], inwards)
+        return zcopy(view(r.zs, i), view(r.zb, i), r.z_s0.at[i], r.z_br.at[i], inwards)
 
     def to_outer(i, src):
-        return zcopy(src.at[i], r.zb.at[i], r.z_s1.at[i], r.z_br.at[i], -inwards)
+        return zcopy(view(src, i), view(r.zb, i), r.z_s1.at[i], r.z_br.at[i], -inwards)
 
     def inward(i, own):
         @pl.when(handed)
         def _():
             to_next(i).wait_recv()
-            r.zs[i] = (own() + r.zu[i].astype(F32)).astype(BF16)
+            view(r.zs, i)[...] = (own() + view(r.zu, i)[...].astype(F32)).astype(BF16)
 
         @pl.when(jnp.logical_not(handed))
         def _():
-            r.zs[i] = own().astype(BF16)
+            view(r.zs, i)[...] = own().astype(BF16)
 
         @pl.when(middle)
         def _():
@@ -534,11 +544,17 @@
         def _():
             to_next(i).start()
 
+    def og_view(i):
+        lo, n = columns(i)
+        k = place(i)
+        at = r.og.at[k // 4, c, k % 4]
+        return at if n == ff else at.at[:, pl.ds(lo, n)]
+
     def og_local(i, src):
-        return pltpu.make_async_copy(src.at[i], r.og.at[i // 4, c, i % 4], r.og_loc.at[i])
+        return pltpu.make_async_copy(view(src, i), og_view(i), r.og_loc.at[i])
 
     def og_across(i, src):
-        return across(src.at[i], r.og.at[i // 4, c, i % 4], r.og_ss.at[i], r.og_rs.at[i])
+        return across(view(src, i), og_view(i), r.og_ss.at[i], r.og_rs.at[i])
 
     def ex_local(q, src):
         return pltpu.make_async_copy(src.at[12 + q, :, pl.ds(512, 128)], r.ex.at[h, c, q], r.ex_loc.at[q])
@@ -560,14 +576,14 @@
             ex_hand_on(q, j).start()
 
     def outward(i):
-        def place(src):
+        def put(src):
             @pl.when(handed)
             def _():
                 to_outer(i, src).start()
 
             og_local(i, src).start()
             og_across(i, src).start()
-            if isinstance(i, int) and i >= 12:
+            if isinstance(i, int) and 12 <= i < 16:
                 ex_local(i - 12, src).start()
                 for j, x in ((3, 0), (1, 0), (2, 0), (0, 1)):
                     ex_plane(i - 12, src, j, x).start()
@@ -577,12 +593,13 @@
         @pl.when(middle)
         def _():
             to_middle(i).wait_send()
-            r.zs[i] = (r.zs[i].astype(F32) + r.zb[i].astype(F32)).astype(BF16)
-            place(r.zs)
+            at = view(r.zs, i)
+            at[...] = (at[...].astype(F32) + view(r.zb, i)[...].astype(F32)).astype(BF16)
+            put(r.zs)
 
         @pl.when(jnp.logical_not(middle))
         def _():
-            place(r.zb)
+            put(r.zb)
 
     def ffn_half(t):
         sl = pl.ds(4 * t, 4)
@@ -596,10 +613,10 @@
         inward(i, lambda: r.gown[i] + r.rf[i].astype(F32))
 
     def within(i, cond, do):
-        if isinstance(i, int) and not 0 <= i < 16:
+        if isinstance(i, int) and not 0 <= i < 17:
             return
 
-        @pl.when((i >= 0) & (i < 16) & cond)
+        @pl.when((i >= 0) & (i < 17) & cond)
         def _():
             do(i)
 
@@ -613,8 +630,8 @@
     def turn(m):
         piece = lambda i: (attention_piece if isinstance(i, int) and i >= 12 else ffn_piece)(i)
         within(m, handed, piece)
-        if isinstance(m, int) and m in (9, 11, 13, 15):
-            within(12 + (m - 9) // 2, outer, piece)
+        if isinstance(m, int) and m in (9, 11, 13, 15, 16):
+            within(12 + (m - 8) // 2, outer, piece)
         if not isinstance(m, int) or m <= 13:
             within(m - 2, middle, outward)
         if isinstance(m, int) and m >= 13:
@@ -645,17 +662,25 @@
         for i in range(k):
             g1 = jnp.where(r.own[k] == r.own[i], k, g1)
 
-    def own_share(to, q):
+    def own_share(to, i):
+        lo, n = columns(i)
+        q = place(i) - 12
         at = pl.ds(q * cr, cr)
         g0 = first_group(to)
-        first = r.ha[g0, at, :].astype(F32) + r.ra[g0, at, :].astype(F32)
+        span = pl.ds(lo, min(n, 512 - lo))
+        first = r.ha[g0, at, span].astype(F32) + r.ra[g0, at, span].astype(F32)
+        if lo + n <= 512:
+            return first
         cols = pl.ds(pl.multiple_of(to * 128, 128), 128)
         second = r.ha[g1, at, cols].astype(F32) + r.ra[g1, at, cols].astype(F32)
         return jnp.concatenate([first, second], axis=1)
 
-    def head_share(j, q):
-        i = 4 * (j - 1) + q
-        return remote(r.sf.at[i], r.rf2.at[i], r.h_ss.at[j, q], r.h_rs.at[j, q], j)
+    def share_slot(ref, j, i):
+        lo, n = columns(i)
+        return ref.at[4 * (j - 1) + place(i) - 12, :, pl.ds(lo, n)]
+
+    def head_share(j, i):
+        return remote(share_slot(r.sf, j, i), share_slot(r.rf2, j, i), r.h_ss.at[j, i - 12], r.h_rs.at[j, i - 12], j)
 
     def attention_sums():
         @pl.loop(0, KV)
@@ -684,20 +709,18 @@
 
         for t in range(3):
             ffn_half(t).wait_send()
-        for q in range(4):
+        for i in range(12, 17):
             for j in (3, 1, 2):
-                r.sf[4 * (j - 1) + q] = own_share(peer_of(h, j), q).astype(BF16)
-                head_share(j, q).start()
+                share_slot(r.sf, j, i)[...] = own_share(peer_of(h, j), i).astype(BF16)
+                head_share(j, i).start()
         turn(KV + 2)
 
     def attention_piece(i):
-        q = i - 12
-
         def own():
-            v = own_share(h, q)
+            v = own_share(h, i)
             for j in (1, 2, 3):
-                head_share(j, q).wait_recv()
-                v = v + r.rf2[4 * (j - 1) + q].astype(F32)
+                head_share(j, i).wait_recv()
+                v = v + share_slot(r.rf2, j, i)[...].astype(F32)
             return v
 
         inward(i, own)
@@ -810,7 +833,7 @@
                 q = r.ql[p, g, k * rows : (k + 1) * rows, :]
                 o = r.ou[g, k * rows : (k + 1) * rows, :]
                 s = nt(q, kv)
-                s = jnp.where(r.bias[...] < 0.0, NEG, s)
+                s = s + r.bias[...]
                 lse = jnp.sum(jnp.where(lane == g * GQ + k, r.lse[p], 0.0), axis=-1, keepdims=True)
                 pr = jnp.exp(s - lse)
                 dpr = nt(o, kv)
@@ -921,7 +944,7 @@
     for cp in gz:
         cp.start()
 
-    for m in range(KV + 3, 21):
+    for m in range(KV + 3, 22):
         turn(m)
         if m == 15:
             final(1, r.gin).send()
@@ -944,15 +967,14 @@
     for cp in gp + gz:
         cp.wait_send()
     for j in (1, 2, 3):
-        for q in range(4):
-            head_share(j, q).wait_send()
+        for i in range(12, 17):
+            head_share(j, i).wait_send()
 
     @pl.loop(0, KV)
     def _(g):
         a_half(g).wait_send()
 
-    @pl.loop(0, 16)
-    def _(i):
+    def settle(i):
         og_local(i, r.zs).wait()
         og_across(i, r.zs).wait_send()
         og_across(i, r.zs).wait_recv()
@@ -964,6 +986,10 @@
         @pl.when(handed)
         def _():
             to_outer(i, r.zs).wait_send()
+
+    pl.loop(0, 12)(settle)
+    for i in range(12, 17):
+        settle(i)
 
     for q in range(4):
         ex_local(q, r.zs).wait()

time: 242 us -> 240 us (level)
  no operation moved by 1% of the time
where the time goes in v2:
time: 240 us; the launch traced here: 238 us
  Pallas kernels  236 us (98%)
    pallas_call x1, Pallas kernels, body(): pl.pallas_call(functools.partial(step_kernel, names, rows, d, ff, nb), ou...  226 us
    pallas_call x1, Pallas kernels, body(): pl.pallas_call(put_kernel, grid=(8,), out_shape=(sd((d, half), BF16), sd(...  9.84 us

profile of v2, /device:TPU:27, one launch (start us, length us, event | category | flops | bytes accessed | tf_op | source)
XLA Modules:
  0.0 237.6 jit_solution(15093237090743348849)
XLA Ops:
  1.3 226.3 %shard_map.221 = (bf16[960,512]{1,0:T(8,128)(2,1)}, bf16[960,512]{1,0:T(8,128)(2,1)}, bf16[4,2,4,120,640]{4,3,2,1,0:T(8,128)(2,1)}, bf16[4,2,4,120,128]{4,3,2,1,0:T(8,128)(2,1)}, f32[2,1,960]{2,1,0:T(1,128)}) custom-call(bf16[960,512]{1,0:T(8,128)(2,1)} %bitcast.22, bf16[960,512]{1,0:T(8,128)(2,1)} %bitcast.23, s32[1]{0:T(128)S(6)} %copy.25.refs_2_, s32[5]{0:T(128)} %own.1, ...), custom_call_target="tpu_custom_call" | custom-call | tf_op jit(solution)/shard_map/pallas_call | solution.py:1046
  227.6 9.8 %shard_map.222 = (bf16[960,512]{1,0:T(8,128)(2,1)}, f32[960,512]{1,0:T(8,128)}, f32[960,384]{1,0:T(8,128)}, f32[960,128]{1,0:T(8,128)}, f32[960,128]{1,0:T(8,128...) custom-call(s32[5]{0:T(128)} %own.1, ...), custom_call_target="tpu_custom_call" | custom-call | tf_op jit(solution)/shard_map/pallas_call | solution.py:1063

commit v3 on v2

--- a/solution.py
+++ b/solution.py
@@ -946,9 +946,9 @@
 
     for m in range(KV + 3, 22):
         turn(m)
-        if m == 15:
+        if m == 13:
             final(1, r.gin).send()
-        if m == 18:
+        if m == 16:
             final(1, r.gin).hand_on()
 
     for cp in gz:
@@ -1012,13 +1012,14 @@
     gw = GQ * HD
     o_out[...] = o[...]
     gin_out[...] = gin[...].astype(F32)
-    gg[...] = og[0].astype(F32)
-    gu[...] = og[1].astype(F32)
-    gd[...] = og[2].astype(F32)
+    wide = lambda x: x.astype(F32).reshape(-1, x.shape[-1])
+    gg[...] = wide(og[0])
+    gu[...] = wide(og[1])
+    gd[...] = wide(og[2])
     ga_out[...] = ga[...]
     gf_out[...] = gf[...]
-    first = og[3, :, 0:512].astype(F32)
-    second = jnp.concatenate([ex[k].astype(F32) for k in range(HEADS)], axis=1)
+    first = wide(og[3])[:, 0:512]
+    second = jnp.concatenate([wide(ex[k]) for k in range(HEADS)], axis=1)
     second = jnp.where(held > 1, second, 0.0)
     for out, lo, width in ((gq, 0, gw), (gk, gw, HD), (gv, gw + HD, HD), (go, gw + 2 * HD, gw)):
         out[...] = jnp.concatenate([first[:, lo : lo + width], second[:, lo : lo + width]], axis=1)
@@ -1057,19 +1058,19 @@
         jnp.asarray(rope_table(2 * half)), w_query, w_key.T, w_value.T, w_output, gate_weight, up_weight, down_weight.T,
     )
     gw, block = GQ * HD, lambda *shape: (lambda index: pl.BlockSpec(shape, index))
-    rowwise = lambda width: block(cr, width)(lambda i: (i, 0))
+    rowwise = lambda width: block(2 * cr, width)(lambda i: (i, 0))
     gains_spec = lambda k: block(None, 1, d)(lambda i: (k, 0, 0))
     gain_out = block(1, d)(lambda i: (0, 0))
     o, gin, gq, gk, gv, go, gg, gu, gd, ga, gf = pl.pallas_call(
         put_kernel,
-        grid=(8,),
+        grid=(4,),
         out_shape=(
             sd((d, half), BF16), sd((d, half), F32), sd((d, 2 * gw), F32), sd((d, 2 * HD), F32), sd((d, 2 * HD), F32),
             sd((d, 2 * gw), F32), sd((d, ff), F32), sd((d, ff), F32), sd((d, ff), F32), sd((1, d), F32), sd((1, d), F32),
         ),
         in_specs=[
-            smem, rowwise(half), rowwise(half), block(4, None, None, cr, ff)(lambda i: (0, i // 4, i % 4, 0, 0)),
-            block(HEADS, None, None, cr, 128)(lambda i: (0, i // 4, i % 4, 0, 0)), gains_spec(0), gains_spec(1),
+            smem, rowwise(half), rowwise(half), block(4, None, 2, cr, ff)(lambda i: (0, i // 2, i % 2, 0, 0)),
+            block(HEADS, None, 2, cr, 128)(lambda i: (0, i // 2, i % 2, 0, 0)), gains_spec(0), gains_spec(1),
         ],
         out_specs=(
             rowwise(half), rowwise(half), rowwise(2 * gw), rowwise(2 * HD), rowwise(2 * HD), rowwise(2 * gw),

time: 240 us -> 239 us (level)
  no operation moved by 1% of the time
where the time goes in v3:
time: 239 us; the launch traced here: 237 us
  Pallas kernels  235 us (98%)
    pallas_call x1, Pallas kernels, body(): pl.pallas_call(functools.partial(step_kernel, names, rows, d, ff, nb), ou...  226 us
    pallas_call x1, Pallas kernels, body(): pl.pallas_call(put_kernel, grid=(4,), out_shape=(sd((d, half), BF16), sd(...  8.94 us

profile of v3, /device:TPU:27, one launch (start us, length us, event | category | flops | bytes accessed | tf_op | source)
XLA Modules:
  0.0 236.7 jit_solution(8166474316506436737)
XLA Ops:
  1.3 226.3 %shard_map.221 = (bf16[960,512]{1,0:T(8,128)(2,1)}, bf16[960,512]{1,0:T(8,128)(2,1)}, bf16[4,2,4,120,640]{4,3,2,1,0:T(8,128)(2,1)}, bf16[4,2,4,120,128]{4,3,2,1,0:T(8,128)(2,1)}, f32[2,1,960]{2,1,0:T(1,128)}) custom-call(bf16[960,512]{1,0:T(8,128)(2,1)} %bitcast.22, bf16[960,512]{1,0:T(8,128)(2,1)} %bitcast.23, s32[1]{0:T(128)S(6)} %copy.25.refs_2_, s32[5]{0:T(128)} %own.1, ...), custom_call_target="tpu_custom_call" | custom-call | tf_op jit(solution)/shard_map/pallas_call | solution.py:1047
  227.6 8.9 %shard_map.222 = (bf16[960,512]{1,0:T(8,128)(2,1)}, f32[960,512]{1,0:T(8,128)}, f32[960,384]{1,0:T(8,128)}, f32[960,128]{1,0:T(8,128)}, f32[960,128]{1,0:T(8,128...) custom-call(s32[5]{0:T(128)} %own.1, ...), custom_call_target="tpu_custom_call" | custom-call | tf_op jit(solution)/shard_map/pallas_call | solution.py:1064

commit v4 on v3

--- a/solution.py
+++ b/solution.py
@@ -773,14 +773,12 @@
             @pl.when(p == 0)
             def _():
                 ffn_half(t).start()
+                if t:
+                    outer_pieces(4 * (t - 1), 4 * t)
 
             ours = nn(lhs[mine_half, :], right)
             for q in range(4):
                 r.gown[4 * t + q] += ours[q * cr : (q + 1) * cr]
-
-        @pl.when(p == 0)
-        def _():
-            outer_pieces(0, 8)
 
         @pl.when(p == 1)
         def _():

time: 239 us -> 239 us (level)
  no operation moved by 1% of the time
where the time goes in v4:
time: 239 us; the launch traced here: 236 us
  Pallas kernels  235 us (98%)
    pallas_call x1, Pallas kernels, body(): pl.pallas_call(functools.partial(step_kernel, names, rows, d, ff, nb), ou...  226 us
    pallas_call x1, Pallas kernels, body(): pl.pallas_call(put_kernel, grid=(4,), out_shape=(sd((d, half), BF16), sd(...  8.94 us

profile of v4, /device:TPU:27, one launch (start us, length us, event | category | flops | bytes accessed | tf_op | source)
XLA Modules:
  0.0 236.3 jit_solution(226219909456642153)
XLA Ops:
  1.3 225.8 %shard_map.221 = (bf16[960,512]{1,0:T(8,128)(2,1)}, bf16[960,512]{1,0:T(8,128)(2,1)}, bf16[4,2,4,120,640]{4,3,2,1,0:T(8,128)(2,1)}, bf16[4,2,4,120,128]{4,3,2,1,0:T(8,128)(2,1)}, f32[2,1,960]{2,1,0:T(1,128)}) custom-call(bf16[960,512]{1,0:T(8,128)(2,1)} %bitcast.22, bf16[960,512]{1,0:T(8,128)(2,1)} %bitcast.23, s32[1]{0:T(128)S(6)} %copy.25.refs_2_, s32[5]{0:T(128)} %own.1, ...), custom_call_target="tpu_custom_call" | custom-call | tf_op jit(solution)/shard_map/pallas_call | solution.py:1045
  227.1 8.9 %shard_map.222 = (bf16[960,512]{1,0:T(8,128)(2,1)}, f32[960,512]{1,0:T(8,128)}, f32[960,384]{1,0:T(8,128)}, f32[960,128]{1,0:T(8,128)}, f32[960,128]{1,0:T(8,128...) custom-call(s32[5]{0:T(128)} %own.1, ...), custom_call_target="tpu_custom_call" | custom-call | tf_op jit(solution)/shard_map/pallas_call | solution.py:1062
